TPU v7x, 32 devices: a whole 2x2x4 slice. The times are simulated.
32 devices in a mesh: shot: 32 (over z, y, x, core), freq: 1.
Axes of the slice: x: 2, y: 2, z: 4, core: 2. Of those that a mesh axis runs over, the one named last changes fastest.
Arguments:
- data: bfloat16 [2, 64, 128, 128], P(None, 'freq', 'shot')
- aperture: int32 [128, 64], P('shot'), may hold values from -1 to 127, as said below
- ops: bfloat16 [8, 64, 64], replicated, may hold values from -0.75 to 0.75
- cable_ops: int32 [2], replicated, may hold values from 0 to 7
Outputs:
- multiples: bfloat16 [2, 64, 128, 128], P(None, 'freq', 'shot')
Inputs may be any that keep to these rules, and one draw needn't show every extreme that they name: `aperture`: each shot's list holds 1 to 64 distinct surface points first, then -1 padding; some shot's list is full.
All inputs are finite; a program needn't handle non-finite values.
Results may differ from a plain program's by a relative error of at most 0.0004.
Values may be sent and summed in bfloat16 or wider, within the bound.
A program may use at most 64 MiB of HBM per device.

v0:
```python
import functools

import jax
import jax.numpy as jnp
from jax import lax
from jax.experimental import pallas as pl
from jax.experimental.pallas import tpu as pltpu
from jax.sharding import PartitionSpec as P

MESH = pl.DeviceIdType.MESH


def kernel(
    n, groups, chunks, finish, data, aperture, ops, cable_ops, out,
    dbuf, apbuf, opsbuf, idbuf, maskbuf, recv, maskrecv, send, back,
    local_sem, recv_sem, send_sem, mask_send_sem, mask_recv_sem, back_send_sem, back_recv_sem, team_sem,
):
    me = lax.axis_index("shot")
    parts, blocks, per, shots, traces = data.shape
    team = n // groups
    freqs = blocks * per
    total, rows = n * shots, team * shots
    cables = cable_ops.shape[0]
    width = ops.shape[1]
    seat = lax.rem(me, team)
    first = me - seat

    flips = []
    for place in (1 << k for k in range(n.bit_length() - 1)):
        flips.append((place, place * (1 - 2 * lax.rem(me // place, 2))))

    def partner(m):
        return me + sum(flip for place, flip in flips if m & place)

    def partner_seat(m):
        return seat + sum(flip for place, flip in flips if m & place and place < team)

    barrier = pltpu.get_barrier_semaphore()
    for m in reversed(range(team, n)):
        pl.semaphore_signal(barrier, inc=1, device_id={"shot": partner(m)}, device_id_type=MESH)

    fetches = [
        pltpu.make_async_copy(aperture, apbuf, local_sem.at[0]),
        pltpu.make_async_copy(ops, opsbuf, local_sem.at[1]),
    ] + [pltpu.make_async_copy(data.at[p], dbuf.at[:, p], local_sem.at[2 + p]) for p in range(parts)]
    fetches.append(pltpu.make_async_copy(cable_ops, idbuf, local_sem.at[2 + parts]))
    for fetch in fetches:
        fetch.start()

    fetches[0].wait()
    lists = apbuf[...]
    surface = lax.broadcasted_iota(jnp.int32, (shots, total), 1)
    found = jnp.zeros((shots, total), jnp.float32)
    for a in range(lists.shape[1]):
        found = jnp.where(lists[:, a : a + 1] == surface, 1.0, found)
    maskbuf[...] = found.astype(jnp.bfloat16)
    for fetch in fetches[1:]:
        fetch.wait()

    pl.semaphore_wait(barrier, n - team)
    pl.semaphore_signal(team_sem, inc=1, device_id={"shot": partner(team)}, device_id_type=MESH)

    def block(chunk, peer_seat):
        return dbuf.at[peer_seat * chunks + chunk]

    def scatter(chunk, peer_seat, peer):
        pltpu.make_async_remote_copy(
            src_ref=block(chunk, peer_seat), dst_ref=recv.at[chunk, me],
            send_sem=send_sem, recv_sem=recv_sem.at[chunk],
            device_id={"shot": peer}, device_id_type=MESH,
        ).start()

    for chunk in range(chunks):
        for m in reversed(range(1, n)):
            if chunk == 0 and m == team - 1:
                pl.semaphore_wait(team_sem, 1)
            if chunk == 0 and m < team:
                pltpu.make_async_remote_copy(
                    src_ref=maskbuf, dst_ref=maskrecv.at[seat],
                    send_sem=mask_send_sem, recv_sem=mask_recv_sem,
                    device_id={"shot": partner(m)}, device_id_type=MESH,
                ).start()
            scatter(chunk, partner_seat(m), partner(m))
        if chunk == 0:
            pltpu.make_async_copy(maskbuf, maskrecv.at[seat], mask_recv_sem).start()
        pltpu.make_async_copy(block(chunk, seat), recv.at[chunk, me], recv_sem.at[chunk]).start()

    lines = []
    for c in range(cables):
        pieces = [jnp.zeros((width, width), jnp.float32)] * cables
        pieces[c] = opsbuf[idbuf[c]].astype(jnp.float32)
        lines.append(jnp.concatenate(pieces, axis=1))
    operator = jnp.concatenate(lines, axis=0).astype(jnp.bfloat16)

    pltpu.make_async_copy(maskrecv, maskrecv, mask_recv_sem).wait()
    mask = maskrecv[...].astype(jnp.float32).reshape(rows, total)

    for chunk in range(chunks):
        pltpu.make_async_copy(recv.at[chunk], recv.at[chunk], recv_sem.at[chunk]).wait()
        for f in range(per):
            real = recv[chunk, :, 0, f].astype(jnp.float32).reshape(total, traces)
            imag = recv[chunk, :, 1, f].astype(jnp.float32).reshape(total, traces)
            if groups == 1:
                own_real, own_imag = real, imag
            else:
                own_real = recv[chunk, pl.ds(first, team), 0, f].astype(jnp.float32).reshape(rows, traces)
                own_imag = recv[chunk, pl.ds(first, team), 1, f].astype(jnp.float32).reshape(rows, traces)
            left = jnp.concatenate([own_real * mask, own_imag * mask], axis=1).astype(jnp.bfloat16)
            right = jnp.concatenate(
                [jnp.concatenate([real, imag], axis=1), jnp.concatenate([-imag, real], axis=1)], axis=0
            ).astype(jnp.bfloat16)
            product = jnp.dot(left, right, preferred_element_type=jnp.float32)
            product = jnp.concatenate([product[:, :traces], product[:, traces:]], axis=0)
            high = product.astype(jnp.bfloat16)
            rest = product - high.astype(jnp.float32)
            middle = rest.astype(jnp.bfloat16)
            low = (rest - middle.astype(jnp.float32)).astype(jnp.bfloat16)
            result = jnp.dot(low, operator, preferred_element_type=jnp.float32)
            result += jnp.dot(middle, operator, preferred_element_type=jnp.float32)
            result += jnp.dot(high, operator, preferred_element_type=jnp.float32)
            result = result.reshape(parts, team, shots, traces)
            for p in range(parts):
                send[chunk, :, p, f] = result[p]

        landing = back.at[seat * chunks + chunk]

        for m in reversed(range(1, team)):
            pltpu.make_async_remote_copy(
                src_ref=send.at[chunk, partner_seat(m)], dst_ref=landing,
                send_sem=back_send_sem, recv_sem=back_recv_sem,
                device_id={"shot": partner(m)}, device_id_type=MESH,
            ).start()
        pltpu.make_async_copy(send.at[chunk, seat], landing, back_recv_sem).start()

    mask_sent = maskrecv.at[pl.ds(0, team - 1)]
    sent = recv.at[:, pl.ds(0, n - 1)]
    back_sent = send.at[:, pl.ds(0, team - 1)]
    pltpu.make_async_copy(mask_sent, mask_sent, mask_send_sem).wait()
    pltpu.make_async_copy(sent, sent, send_sem).wait()
    pltpu.make_async_copy(back, back, back_recv_sem).wait()
    if finish:
        predicted = back[...]
        energy = jnp.sum(jnp.sum(predicted * predicted, axis=(0, 1, 2)), axis=1, keepdims=True)
        scale = lax.rsqrt(energy / (2.0 * freqs * traces) + 1e-06)
        for p in range(parts):
            out[p] = (back[:, p] * scale[None, None]).astype(out.dtype)
    pltpu.make_async_copy(back_sent, back_sent, back_send_sem).wait()


GROUPS = 2
CHUNKS = 2


def per_device(n, bands, data, aperture, ops, cable_ops):
    parts, freqs, shots, traces = data.shape
    groups, chunks = GROUPS, CHUNKS
    team = n // groups
    per = freqs // (team * chunks)
    finish = bands == 1
    dma = pltpu.SemaphoreType.DMA
    blocks = team * chunks
    held = (blocks, parts, per, shots, traces)
    shape = (parts, blocks, per, shots, traces) if finish else held
    scratch = [
        pltpu.VMEM(held, data.dtype),
        pltpu.VMEM(aperture.shape, aperture.dtype),
        pltpu.VMEM(ops.shape, ops.dtype),
        pltpu.SMEM(cable_ops.shape, cable_ops.dtype),
        pltpu.VMEM((shots, n * shots), jnp.bfloat16),
        pltpu.VMEM((chunks, n, parts, per, shots, traces), jnp.bfloat16),
        pltpu.VMEM((team, shots, n * shots), jnp.bfloat16),
        pltpu.VMEM((chunks, team, parts, per, shots, traces), jnp.float32),
    ]
    sems = [dma((3 + parts,)), dma((chunks,))] + [dma] * 5 + [pltpu.SemaphoreType.REGULAR]
    anywhere = pl.BlockSpec(memory_space=pl.ANY)
    body = functools.partial(kernel, n, groups, chunks, finish)
    if finish:
        scratch.append(pltpu.VMEM(held, jnp.float32))
        out_dtype = jnp.bfloat16
    else:
        inner = body

        def body(data, aperture, ops, cable_ops, out, *rest):
            place = len(scratch)
            inner(data, aperture, ops, cable_ops, out, *rest[:place], out, *rest[place:])

        out_dtype = jnp.float32
    result = pl.pallas_call(
        body,
        out_shape=pltpu.VMEM(shape, out_dtype),
        in_specs=[anywhere] * 4,
        out_specs=pl.BlockSpec(memory_space=pltpu.VMEM),
        scratch_shapes=scratch + sems,
        compiler_params=pltpu.CompilerParams(collective_id=0, has_side_effects=True),
        name="predict",
    )(data.reshape(parts, blocks, per, shots, traces), aperture, ops, cable_ops)
    if finish:
        return result.reshape(data.shape)
    result = jnp.swapaxes(result, 0, 1).reshape(data.shape)
    energy = lax.psum(jnp.sum(result * result, axis=(0, 1, 3)), "freq")
    scale = lax.rsqrt(energy / (2.0 * freqs * bands * traces) + 1e-06)
    return (result * scale[None, None, :, None]).astype(jnp.bfloat16)


def solution(mesh):
    return jax.shard_map(
        functools.partial(per_device, mesh.shape["shot"], mesh.shape["freq"]),
        mesh=mesh,
        in_specs=(P(None, "freq", "shot", None), P("shot", None), P(), P()),
        out_specs=P(None, "freq", "shot", None),
        check_vma=False,
    )
```

profile of v0, /device:TPU:0, one launch (start us, length us, event | category | flops | bytes accessed | tf_op | source)
XLA Modules:
  0.0 19.2 jit_solution(16090755319827850833)
XLA Ops:
  0.0 18.6 %predict.1 = bf16[2,32,2,4,128]{4,3,2,1,0:T(4,128)(2,1)S(1)} custom-call(bf16[2,32,2,4,128]{4,3,2,1,0:T(4,128)(2,1)} %bitcast.3, s32[4,64]{1,0:T(4,128)} %aperture.1, bf16[8,64,64]{2,1,0:T(8,128)(2,1)} %ops.1, s32[2]{0:T(128)} %cable_ops.1), custom_call_target="tpu_custom_call" | custom-call | tf_op jit(solution)/shard_map/predict/pallas_call | solution.py:188
  18.6 0.7 %copy.6 = bf16[2,64,4,128]{3,2,1,0:T(4,128)(2,1)} copy(bf16[2,64,4,128]{3,2,1,0:T(4,128)(2,1)S(1)} %bitcast.2) | data formatting | bytes 262144
where the time goes:
time: 19.4 us; the launch traced here: 19.2 us
  Pallas kernels  18.6 us (96%)
  local copies, waits for them, and re-layouts  0.66 us (3%)
    pallas_call x1, Pallas kernels, per_device(): pl.pallas_call(body, out_shape=pltpu.VMEM(shape, out_dtype), in_specs=[an...  18.6 us
    unnamed x1, local copies, waits for them, and re-layouts  0.66 us

commit v1 on v0

v1 whole, which is shorter than its diff:
```python
import functools

import jax
import jax.numpy as jnp
from jax import lax
from jax.experimental import pallas as pl
from jax.experimental.pallas import tpu as pltpu
from jax.sharding import PartitionSpec as P

MESH = pl.DeviceIdType.MESH

def kernel(n, sizes, finish, data, aperture, ops, cable_ops, out, *scratch):
    chunks = len(sizes)
    dbufs, recvs = scratch[:chunks], scratch[chunks : 2 * chunks]
    sends, backs = scratch[2 * chunks : 3 * chunks], scratch[3 * chunks : 4 * chunks]
    apbuf, opsbuf, idbuf, tally = scratch[4 * chunks : 4 * chunks + 4]
    local_sem, recv_sem, send_sem, back_send_sem, back_recv_sem, in_sem, team_sem = scratch[4 * chunks + 4 :]
    me = lax.axis_index("shot")
    parts, team, freqs, shots, traces = data.shape
    plane = team // 2
    total, rows = n * shots, team * shots
    cables = cable_ops.shape[0]
    width = ops.shape[1]
    seat = lax.rem(me, team)
    first = me - seat
    upper = me // team
    spot = lax.rem(me, plane)

    flips = []
    for place in (1 << k for k in range(n.bit_length() - 1)):
        flips.append((place, place * (1 - 2 * lax.rem(me // place, 2))))

    def flip(base, m):
        return base + sum(step for place, step in flips if m & place)

    def signal(sem, device):
        pl.semaphore_signal(sem, inc=1, device_id={"shot": device}, device_id_type=MESH)

    def settle(sem, blocks):
        amount = tally.at[pl.ds(0, blocks)]
        pltpu.make_async_copy(amount, amount, sem).wait()

    offsets = [sum(sizes[:c]) for c in range(chunks)]
    fetches = []
    for c in range(chunks):
        for p in range(parts):
            fetches.append(pltpu.make_async_copy(
                data.at[p, :, pl.ds(offsets[c], sizes[c])],
                dbufs[c].at[:, pl.ds(p * sizes[c], sizes[c])],
                local_sem.at[3 + c * parts + p],
            ))
    fetch_ap = pltpu.make_async_copy(aperture, apbuf, local_sem.at[0])
    fetch_ops = pltpu.make_async_copy(ops, opsbuf, local_sem.at[1])
    fetch_ids = pltpu.make_async_copy(cable_ops, idbuf, local_sem.at[2])
    for fetch in fetches:
        fetch.start()
    fetch_ap.start()

    barrier = pltpu.get_barrier_semaphore()

    @pl.when(upper == 0)
    def _():
        for m in reversed(range(1, n)):
            signal(barrier, flip(me, m))

    fetch_ops.start()
    fetch_ids.start()

    def note():
        fetch_ap.wait()
        lists = apbuf[...]
        surface = lax.broadcasted_iota(jnp.int32, (shots, total), 1)
        found = jnp.zeros((shots, total), jnp.float32)
        for a in range(lists.shape[1]):
            found = jnp.where(lists[:, a : a + 1] == surface, 1.0, found)
        found = found.astype(jnp.bfloat16)
        for k in range(team):
            dbufs[0][k, parts * sizes[0]] = found

    def scatter(c, device, device_seat, near):
        extent = parts * sizes[c] + (c == 0 and near)
        pltpu.make_async_remote_copy(
            src_ref=dbufs[c].at[device_seat, pl.ds(0, extent)],
            dst_ref=recvs[c].at[me, pl.ds(0, extent)],
            send_sem=send_sem.at[c], recv_sem=recv_sem.at[c],
            device_id={"shot": device}, device_id_type=MESH,
        ).start()

    def scatter_near(c):
        for m in reversed(range(1, team)):
            scatter(c, flip(me, m), flip(seat, m), True)
        pltpu.make_async_copy(dbufs[c].at[seat], recvs[c].at[me], recv_sem.at[c]).start()

    level = lax.rem(me // plane, 2)

    def scatter_far(c, *levels):
        low = (1 - upper) * team
        for m in reversed(range(plane)):
            for step in levels:
                place = flip(spot, m) + step * plane
                scatter(c, low + place, place, False)

    @pl.when(upper == 0)
    def _():
        note()
        for fetch in fetches:
            fetch.wait()
        pl.semaphore_wait(barrier, team - 1)
        for c in range(chunks):
            scatter_near(c)
        pl.semaphore_wait(in_sem.at[0], plane)
        scatter_far(0, 0)
        pl.semaphore_wait(in_sem.at[1], plane)

        @pl.when(level == 1)
        def _():
            for step in range(2):
                signal(team_sem, team + step * plane + spot)

        scatter_far(0, 1)
        for c in range(1, chunks):
            scatter_far(c, 1, 0)

    @pl.when(upper == 1)
    def _():
        for fetch in fetches:
            fetch.wait()
        pl.semaphore_wait(barrier, team)

        def announce():
            for m in reversed(range(team, n)):
                signal(in_sem.at[(me - team) // plane], flip(me, m))

        announce()
        for c in range(chunks):
            scatter_far(c, 0, 1)
        note()
        pl.semaphore_wait(team_sem, 1)
        for c in range(chunks):
            scatter_near(c)

    fetch_ops.wait()
    fetch_ids.wait()
    lines = []
    for c in range(cables):
        pieces = [jnp.zeros((width, width), jnp.float32)] * cables
        pieces[c] = opsbuf[idbuf[c]].astype(jnp.float32)
        lines.append(jnp.concatenate(pieces, axis=1))
    operator = jnp.concatenate(lines, axis=0).astype(jnp.bfloat16)

    mask = None
    for c in range(chunks):
        per = sizes[c]
        if c == 0:
            settle(recv_sem.at[0], n * parts * per + team)
        else:
            pltpu.make_async_copy(recvs[c], recvs[c], recv_sem.at[c]).wait()
        if c == 0:
            mask = recvs[0][pl.ds(first, team), parts * per].astype(jnp.float32).reshape(rows, total)
        for f in range(per):
            real = recvs[c][:, f].astype(jnp.float32).reshape(total, traces)
            imag = recvs[c][:, per + f].astype(jnp.float32).reshape(total, traces)
            own_real = recvs[c][pl.ds(first, team), f].astype(jnp.float32).reshape(rows, traces)
            own_imag = recvs[c][pl.ds(first, team), per + f].astype(jnp.float32).reshape(rows, traces)
            left = jnp.concatenate([own_real * mask, own_imag * mask], axis=1).astype(jnp.bfloat16)
            right = jnp.concatenate(
                [jnp.concatenate([real, imag], axis=1), jnp.concatenate([-imag, real], axis=1)], axis=0
            ).astype(jnp.bfloat16)
            product = jnp.dot(left, right, preferred_element_type=jnp.float32)
            product = jnp.concatenate([product[:, :traces], product[:, traces:]], axis=0)
            high = product.astype(jnp.bfloat16)
            rest = product - high.astype(jnp.float32)
            middle = rest.astype(jnp.bfloat16)
            low = (rest - middle.astype(jnp.float32)).astype(jnp.bfloat16)
            result = jnp.dot(low, operator, preferred_element_type=jnp.float32)
            result += jnp.dot(middle, operator, preferred_element_type=jnp.float32)
            result += jnp.dot(high, operator, preferred_element_type=jnp.float32)
            result = result.reshape(parts, team, shots, traces)
            for p in range(parts):
                sends[c][:, p, f] = result[p]

        landing = backs[c].at[seat]
        for m in reversed(range(1, team)):
            pltpu.make_async_remote_copy(
                src_ref=sends[c].at[flip(seat, m)], dst_ref=landing,
                send_sem=back_send_sem.at[c], recv_sem=back_recv_sem.at[c],
                device_id={"shot": flip(me, m)}, device_id_type=MESH,
            ).start()
        pltpu.make_async_copy(sends[c].at[seat], landing, back_recv_sem.at[c]).start()

    for c in range(chunks):
        settle(send_sem.at[c], (n - 1) * parts * sizes[c] + (team - 1) * (c == 0))
    energy = 0.0
    for c in range(chunks):
        pltpu.make_async_copy(backs[c], backs[c], back_recv_sem.at[c]).wait()
        if finish:
            predicted = backs[c][...]
            energy += jnp.sum(predicted * predicted, axis=(0, 1, 2))
    if finish:
        energy = jnp.sum(energy, axis=1, keepdims=True)
        scale = lax.rsqrt(energy / (2.0 * team * freqs * traces) + 1e-06)
    for c in range(chunks):
        for p in range(parts):
            value = backs[c][:, p]
            if finish:
                value = value * scale[None, None]
            out[p, :, pl.ds(offsets[c], sizes[c])] = value.astype(out.dtype)
    for c in range(chunks):
        sent = sends[c].at[pl.ds(0, team - 1)]
        pltpu.make_async_copy(sent, sent, back_send_sem.at[c]).wait()


def per_device(n, bands, data, aperture, ops, cable_ops):
    parts, freqs, shots, traces = data.shape
    team = n // 2
    per = freqs // team
    sizes = [1] * per
    chunks = len(sizes)
    finish = bands == 1
    dma = pltpu.SemaphoreType.DMA
    regular = pltpu.SemaphoreType.REGULAR
    vmem = pltpu.VMEM
    scratch = [vmem((team, parts * s + (c == 0), shots, traces), data.dtype) for c, s in enumerate(sizes)]
    scratch += [vmem((n, parts * s + (c == 0), shots, traces), data.dtype) for c, s in enumerate(sizes)]
    scratch += [vmem((team, parts, s, shots, traces), jnp.float32) for s in sizes] * 2
    scratch += [
        vmem(aperture.shape, aperture.dtype),
        vmem(ops.shape, ops.dtype),
        pltpu.SMEM(cable_ops.shape, cable_ops.dtype),
        vmem((n * parts * max(sizes) + team, shots, traces), data.dtype),
        dma((3 + parts * chunks,)), dma((chunks,)), dma((chunks,)), dma((chunks,)), dma((chunks,)),
        regular((2,)), regular,
    ]
    anywhere = pl.BlockSpec(memory_space=pl.ANY)
    result = pl.pallas_call(
        functools.partial(kernel, n, sizes, finish),
        out_shape=vmem((parts, team, per, shots, traces), jnp.bfloat16 if finish else jnp.float32),
        in_specs=[anywhere] * 4,
        out_specs=pl.BlockSpec(memory_space=vmem),
        scratch_shapes=scratch,
        compiler_params=pltpu.CompilerParams(collective_id=0, has_side_effects=True),
        name="predict",
    )(data.reshape(parts, team, per, shots, traces), aperture, ops, cable_ops)
    result = result.reshape(data.shape)
    if finish:
        return result
    energy = lax.psum(jnp.sum(result * result, axis=(0, 1, 3)), "freq")
    scale = lax.rsqrt(energy / (2.0 * freqs * bands * traces) + 1e-06)
    return (result * scale[None, None, :, None]).astype(jnp.bfloat16)


def solution(mesh):
    return jax.shard_map(
        functools.partial(per_device, mesh.shape["shot"], mesh.shape["freq"]),
        mesh=mesh,
        in_specs=(P(None, "freq", "shot", None), P("shot", None), P(), P()),
        out_specs=P(None, "freq", "shot", None),
        check_vma=False,
    )
```

time: 19.4 us -> 18.5 us (0.954)
  Pallas kernels: 18.6 us -> 17.6 us
    pallas_call x1, Pallas kernels: 18.6 us -> 17.6 us  [per_device(): pl.pallas_call(functools.partial(kernel, n, sizes, finish), out_shape=vme...]
where the time goes in v1:
time: 18.5 us; the launch traced here: 18.2 us
  Pallas kernels  17.6 us (95%)
  local copies, waits for them, and re-layouts  0.66 us (4%)
    pallas_call x1, Pallas kernels, per_device(): pl.pallas_call(functools.partial(kernel, n, sizes, finish), out_shape=vme...  17.6 us
    unnamed x1, local copies, waits for them, and re-layouts  0.66 us

profile of v1, /device:TPU:0, one launch (start us, length us, event | category | flops | bytes accessed | tf_op | source)
XLA Modules:
  0.0 18.2 jit_solution(8526319647247147679)
XLA Ops:
  0.0 17.6 %predict.1 = bf16[2,16,4,4,128]{4,3,2,1,0:T(4,128)(2,1)S(1)} custom-call(bf16[2,16,4,4,128]{4,3,2,1,0:T(4,128)(2,1)} %bitcast.3, s32[4,64]{1,0:T(4,128)} %aperture.1, bf16[8,64,64]{2,1,0:T(8,128)(2,1)} %ops.1, s32[2]{0:T(128)} %cable_ops.1), custom_call_target="tpu_custom_call" | custom-call | tf_op jit(solution)/shard_map/predict/pallas_call | solution.py:235
  17.6 0.7 %copy.6 = bf16[2,64,4,128]{3,2,1,0:T(4,128)(2,1)} copy(bf16[2,64,4,128]{3,2,1,0:T(4,128)(2,1)S(1)} %bitcast.2) | data formatting | bytes 262144

commit v2 on v1

v2 whole, which is shorter than its diff:
```python
import functools

import jax
import jax.numpy as jnp
from jax import lax
from jax.experimental import pallas as pl
from jax.experimental.pallas import tpu as pltpu
from jax.sharding import PartitionSpec as P

MESH = pl.DeviceIdType.MESH
PIECES = 2


def kernel(n, sizes, finish, data, aperture, ops, cable_ops, out, *scratch):
    chunks = len(sizes)
    dbufs, recvs = scratch[:chunks], scratch[chunks : 2 * chunks]
    sends, backs = scratch[2 * chunks : 3 * chunks], scratch[3 * chunks : 4 * chunks]
    apbuf, opsbuf, idbuf, lbuf, wbuf, tally = scratch[4 * chunks : 4 * chunks + 6]
    local_sem, recv_sem, send_sem, back_send_sem, back_recv_sem, in_sem, team_sem, group_sem = scratch[4 * chunks + 6 :]
    me = lax.axis_index("shot")
    parts, team, freqs, shots, traces = data.shape
    plane = team // 2
    total, rows = n * shots, team * shots
    cables = cable_ops.shape[0]
    width = ops.shape[1]
    seat = lax.rem(me, team)
    first = me - seat
    upper = me // team
    spot = lax.rem(me, plane)

    flips = []
    for place in (1 << k for k in range(n.bit_length() - 1)):
        flips.append((place, place * (1 - 2 * lax.rem(me // place, 2))))

    def flip(base, m):
        return base + sum(step for place, step in flips if m & place)

    def signal(sem, device):
        pl.semaphore_signal(sem, inc=1, device_id={"shot": device}, device_id_type=MESH)

    def settle_blocks(sem, blocks):
        amount = tally.at[pl.ds(0, blocks)]
        pltpu.make_async_copy(amount, amount, sem).wait()

    def settle(sem, c, near, peers):
        extent = parts * sizes[c] + (c == 0 and near)
        amount = recvs[c].at[pl.ds(0, peers), pl.ds(0, extent)]
        pltpu.make_async_copy(amount, amount, sem).wait()

    offsets = [sum(sizes[:c]) for c in range(chunks)]
    fetches = [
        pltpu.make_async_copy(
            data.at[p, :, pl.ds(offsets[c], sizes[c])],
            dbufs[c].at[:, pl.ds(p * sizes[c], sizes[c])],
            local_sem.at[3],
        )
        for c in range(chunks)
        for p in range(parts)
    ]
    fetch_ap = pltpu.make_async_copy(aperture, apbuf, local_sem.at[0])
    fetch_ops = pltpu.make_async_copy(ops, opsbuf, local_sem.at[1])
    fetch_ids = pltpu.make_async_copy(cable_ops, idbuf, local_sem.at[2])

    barrier = pltpu.get_barrier_semaphore()

    level = lax.rem(me // plane, 2)
    groups = [m for m in range(plane) if not m & 1]

    def opposite(step):
        return (1 - upper) * team + step * plane + spot

    diagonal = groups[-1]

    @pl.when(upper == 0)
    def _():
        for m in sorted(range(1, n), key=lambda m: (m < team, m & diagonal != diagonal, -m)):
            signal(barrier, flip(me, m))

    for fetch in fetches:
        fetch.start()
    fetch_ap.start()

    @pl.when(level * upper == 1)
    def _():
        for step in range(2):
            for m in range(2):
                signal(barrier, flip(opposite(step), m))

    fetch_ops.start()
    fetch_ids.start()

    def note():
        fetch_ap.wait()
        lists = apbuf[...]
        surface = lax.broadcasted_iota(jnp.int32, (shots, total), 1)
        found = jnp.zeros((shots, total), jnp.float32)
        for a in range(lists.shape[1]):
            found = jnp.where(lists[:, a : a + 1] == surface, 1.0, found)
        found = found.astype(jnp.bfloat16)
        for k in range(team):
            dbufs[0][k, parts * sizes[0]] = found

    def scatter(c, device, device_seat, near):
        extent = parts * sizes[c] + (c == 0 and near)
        pltpu.make_async_remote_copy(
            src_ref=dbufs[c].at[device_seat, pl.ds(0, extent)],
            dst_ref=recvs[c].at[me, pl.ds(0, extent)],
            send_sem=send_sem, recv_sem=recv_sem.at[int(near), c],
            device_id={"shot": device}, device_id_type=MESH,
        ).start()

    def scatter_near(c):
        for m in reversed(range(1, team)):
            scatter(c, flip(me, m), flip(seat, m), True)
        pltpu.make_async_copy(dbufs[c].at[seat], recvs[c].at[me], recv_sem.at[1, c]).start()

    def scatter_far(c, *chosen):
        for g in chosen:
            for m in (g + 1, g):
                for step in range(2):
                    place = flip(spot, m) + step * plane
                    scatter(c, (1 - upper) * team + place, place, False)

    @pl.when(upper == 0)
    def _():
        note()
        pltpu.make_async_copy(data, data, local_sem.at[3]).wait()
        pl.semaphore_wait(barrier, team + 1)
        scatter_near(0)
        pl.semaphore_wait(in_sem, 2)
        for g in groups[1:]:
            signal(group_sem.at[g // 2 - 1], flip(me, g))
        for c in range(1, chunks):
            scatter_near(c)
        for c in range(chunks):
            scatter_far(c, 0)
        for g in groups[1:]:
            pl.semaphore_wait(group_sem.at[g // 2 - 1], 1)
            if g == groups[-1]:

                @pl.when(level == 1)
                def _():
                    for step in range(2):
                        signal(team_sem, opposite(step))

            scatter_far(0, g)
        for c in range(1, chunks):
            scatter_far(c, *reversed(groups[1:]))

    @pl.when(upper == 1)
    def _():
        pltpu.make_async_copy(data, data, local_sem.at[3]).wait()
        pl.semaphore_wait(barrier, team)

        @pl.when(level == 0)
        def _():
            for step in range(2):
                for m in range(2):
                    signal(in_sem, flip(opposite(step), m))

        for c in range(chunks - 1):
            scatter_far(c, *reversed(groups))
            if c == 1:
                note()
        if chunks < 3:
            note()
        pl.semaphore_wait(team_sem, 1)
        scatter_near(0)
        scatter_far(chunks - 1, *reversed(groups))
        for c in range(1, chunks):
            scatter_near(c)

    fetch_ops.wait()
    fetch_ids.wait()
    lines = []
    for c in range(cables):
        pieces = [jnp.zeros((width, width), jnp.float32)] * cables
        pieces[c] = opsbuf[idbuf[c]].astype(jnp.float32)
        lines.append(jnp.concatenate(pieces, axis=1))
    operator = jnp.concatenate([jnp.concatenate(lines, axis=0).astype(jnp.bfloat16)] * PIECES, axis=0)

    def flat(c, start, f):
        return recvs[c][pl.ds(start, team), f].astype(jnp.float32).reshape(rows, traces)

    def place(c, start, f, real, imag):
        base = pl.multiple_of(start * shots, rows)
        wbuf[offsets[c] + f, pl.ds(base, rows)] = real.astype(jnp.bfloat16)
        wbuf[offsets[c] + f, pl.ds(base + total, rows)] = imag.astype(jnp.bfloat16)

    masks = []

    def prepare(c):
        per = sizes[c]
        settle(recv_sem.at[1, c], c, True, team)
        if c == 0:
            masks.append(recvs[0][pl.ds(first, team), parts * per].astype(jnp.float32).reshape(rows, total))
        for f in range(per):
            real, imag = flat(c, first, f), flat(c, first, per + f)
            place(c, first, f, real, imag)
            real, imag = real * masks[0], imag * masks[0]
            lbuf[offsets[c] + f] = jnp.concatenate(
                [jnp.concatenate([real, -imag], axis=1), jnp.concatenate([imag, real], axis=1)], axis=0
            ).astype(jnp.bfloat16)

    def finish_chunk(c):
        per = sizes[c]
        settle(recv_sem.at[0, c], c, False, team)
        for f in range(per):
            place(c, team - first, f, flat(c, team - first, f), flat(c, team - first, per + f))
            rest = jnp.dot(lbuf[offsets[c] + f], wbuf[offsets[c] + f], preferred_element_type=jnp.float32)
            pieces = []
            for piece in range(PIECES):
                pieces.append(rest.astype(jnp.bfloat16))
                rest = rest - pieces[-1].astype(jnp.float32)
            result = jnp.dot(jnp.concatenate(pieces[::-1], axis=1), operator, preferred_element_type=jnp.float32)
            result = result.reshape(parts, team, shots, traces)
            for p in range(parts):
                sends[c][:, p, f] = result[p]

        landing = backs[c].at[seat]
        for m in reversed(range(1, team)):
            pltpu.make_async_remote_copy(
                src_ref=sends[c].at[flip(seat, m)], dst_ref=landing,
                send_sem=back_send_sem, recv_sem=back_recv_sem.at[max(0, c + 2 - chunks)],
                device_id={"shot": flip(me, m)}, device_id_type=MESH,
            ).start()
        pltpu.make_async_copy(sends[c].at[seat], landing, back_recv_sem.at[max(0, c + 2 - chunks)]).start()

    for c in range(-2, chunks):
        if c >= 0:
            finish_chunk(c)
        if c + 2 < chunks:
            prepare(c + 2)

    settle_blocks(send_sem, (n - 1) * parts * freqs + team - 1)

    def wait_back(which, c_from, c_to):
        total_f = sum(sizes[c_from:c_to])
        settle_blocks(back_recv_sem.at[which], 2 * team * parts * total_f)

    def power(c):
        predicted = backs[c][...]
        return jnp.sum(predicted * predicted, axis=(0, 1, 2))

    energy = jnp.zeros((shots, traces), jnp.float32)
    if chunks > 1:
        wait_back(0, 0, chunks - 1)
        for c in range(chunks - 1):
            energy += power(c)
    wait_back(1, chunks - 1, chunks)
    energy = jnp.sum(energy + power(chunks - 1), axis=1, keepdims=True)
    scale = lax.rsqrt(energy / (2.0 * team * freqs * traces) + 1e-06)
    for c in range(chunks):
        for p in range(parts):
            value = backs[c][:, p]
            if finish:
                value = value * scale[None, None]
            out[p, :, pl.ds(offsets[c], sizes[c])] = value.astype(out.dtype)
    settle_blocks(back_send_sem, 2 * (team - 1) * parts * freqs)


def per_device(n, bands, data, aperture, ops, cable_ops):
    parts, freqs, shots, traces = data.shape
    team = n // 2
    per = freqs // team
    sizes = [1] * per
    chunks = len(sizes)
    finish = bands == 1
    dma = pltpu.SemaphoreType.DMA
    regular = pltpu.SemaphoreType.REGULAR
    vmem = pltpu.VMEM
    scratch = [vmem((team, parts * s + (c == 0), shots, traces), data.dtype) for c, s in enumerate(sizes)]
    scratch += [vmem((n, parts * s + (c == 0), shots, traces), data.dtype) for c, s in enumerate(sizes)]
    scratch += [vmem((team, parts, s, shots, traces), jnp.float32) for s in sizes] * 2
    scratch += [
        vmem(aperture.shape, aperture.dtype),
        vmem(ops.shape, ops.dtype),
        pltpu.SMEM(cable_ops.shape, cable_ops.dtype),
        vmem((per, parts * team * shots, parts * traces), data.dtype),
        vmem((per, parts * n * shots, traces), data.dtype),
        vmem((n * parts * per + team, shots, traces), data.dtype),
        dma((4,)), dma((2, chunks)), dma, dma, dma((2,)),
        regular, regular, regular((n // 8 - 1,)),
    ]
    anywhere = pl.BlockSpec(memory_space=pl.ANY)
    result = pl.pallas_call(
        functools.partial(kernel, n, sizes, finish),
        out_shape=vmem((parts, team, per, shots, traces), jnp.bfloat16 if finish else jnp.float32),
        in_specs=[anywhere] * 4,
        out_specs=pl.BlockSpec(memory_space=vmem),
        scratch_shapes=scratch,
        compiler_params=pltpu.CompilerParams(collective_id=0, has_side_effects=True),
        name="predict",
    )(data.reshape(parts, team, per, shots, traces), aperture, ops, cable_ops)
    result = result.reshape(data.shape)
    if finish:
        return result
    energy = lax.psum(jnp.sum(result * result, axis=(0, 1, 3)), "freq")
    scale = lax.rsqrt(energy / (2.0 * freqs * bands * traces) + 1e-06)
    return (result * scale[None, None, :, None]).astype(jnp.bfloat16)


def solution(mesh):
    return jax.shard_map(
        functools.partial(per_device, mesh.shape["shot"], mesh.shape["freq"]),
        mesh=mesh,
        in_specs=(P(None, "freq", "shot", None), P("shot", None), P(), P()),
        out_specs=P(None, "freq", "shot", None),
        check_vma=False,
    )
```

time: 18.5 us -> 18 us (0.973)
  Pallas kernels: 17.6 us -> 17.2 us
    pallas_call x1, Pallas kernels: 17.6 us -> 17.2 us  [per_device(): pl.pallas_call(functools.partial(kernel, n, sizes, finish), out_shape=vme...]
where the time goes in v2:
time: 18 us; the launch traced here: 17.8 us
  Pallas kernels  17.2 us (96%)
  local copies, waits for them, and re-layouts  0.66 us (4%)
    pallas_call x1, Pallas kernels, per_device(): pl.pallas_call(functools.partial(kernel, n, sizes, finish), out_shape=vme...  17.2 us
    unnamed x1, local copies, waits for them, and re-layouts  0.66 us

profile of v2, /device:TPU:0, one launch (start us, length us, event | category | flops | bytes accessed | tf_op | source)
XLA Modules:
  0.0 17.8 jit_solution(4625369310803533430)
XLA Ops:
  0.0 17.2 %predict.1 = bf16[2,16,4,4,128]{4,3,2,1,0:T(4,128)(2,1)S(1)} custom-call(bf16[2,16,4,4,128]{4,3,2,1,0:T(4,128)(2,1)} %bitcast.3, s32[4,64]{1,0:T(4,128)} %aperture.1, bf16[8,64,64]{2,1,0:T(8,128)(2,1)} %ops.1, s32[2]{0:T(128)} %cable_ops.1), custom_call_target="tpu_custom_call" | custom-call | tf_op jit(solution)/shard_map/predict/pallas_call | solution.py:286
  17.2 0.7 %copy.6 = bf16[2,64,4,128]{3,2,1,0:T(4,128)(2,1)} copy(bf16[2,64,4,128]{3,2,1,0:T(4,128)(2,1)S(1)} %bitcast.2) | data formatting | bytes 262144

commit v3 on v2

--- a/solution.py
+++ b/solution.py
@@ -8,7 +8,7 @@
 from jax.sharding import PartitionSpec as P
 
 MESH = pl.DeviceIdType.MESH
-PIECES = 2
+PIECES = 3
 
 
 def kernel(n, sizes, finish, data, aperture, ops, cable_ops, out, *scratch):

time: 18 us -> 18 us (level)
  no operation moved by 1% of the time
where the time goes in v3:
time: 18 us; the launch traced here: 17.9 us
  Pallas kernels  17.2 us (96%)
  local copies, waits for them, and re-layouts  0.66 us (4%)
    pallas_call x1, Pallas kernels, per_device(): pl.pallas_call(functools.partial(kernel, n, sizes, finish), out_shape=vme...  17.2 us
    unnamed x1, local copies, waits for them, and re-layouts  0.66 us

profile of v3, /device:TPU:0, one launch (start us, length us, event | category | flops | bytes accessed | tf_op | source)
XLA Modules:
  0.0 17.9 jit_solution(2564554484160386463)
XLA Ops:
  0.0 17.2 %predict.1 = bf16[2,16,4,4,128]{4,3,2,1,0:T(4,128)(2,1)S(1)} custom-call(bf16[2,16,4,4,128]{4,3,2,1,0:T(4,128)(2,1)} %bitcast.3, s32[4,64]{1,0:T(4,128)} %aperture.1, bf16[8,64,64]{2,1,0:T(8,128)(2,1)} %ops.1, s32[2]{0:T(128)} %cable_ops.1), custom_call_target="tpu_custom_call" | custom-call | tf_op jit(solution)/shard_map/predict/pallas_call | solution.py:286
  17.2 0.7 %copy.6 = bf16[2,64,4,128]{3,2,1,0:T(4,128)(2,1)} copy(bf16[2,64,4,128]{3,2,1,0:T(4,128)(2,1)S(1)} %bitcast.2) | data formatting | bytes 262144

commit v4 on v3

--- a/solution.py
+++ b/solution.py
@@ -16,7 +16,7 @@
     dbufs, recvs = scratch[:chunks], scratch[chunks : 2 * chunks]
     sends, backs = scratch[2 * chunks : 3 * chunks], scratch[3 * chunks : 4 * chunks]
     apbuf, opsbuf, idbuf, lbuf, wbuf, tally = scratch[4 * chunks : 4 * chunks + 6]
-    local_sem, recv_sem, send_sem, back_send_sem, back_recv_sem, in_sem, team_sem, group_sem = scratch[4 * chunks + 6 :]
+    local_sem, recv_sem, send_sem, back_send_sem, back_recv_sem, in_sem, col_sem, team_sem, group_sem = scratch[4 * chunks + 6 :]
     me = lax.axis_index("shot")
     parts, team, freqs, shots, traces = data.shape
     plane = team // 2
@@ -82,9 +82,8 @@
 
     @pl.when(level * upper == 1)
     def _():
-        for step in range(2):
-            for m in range(2):
-                signal(barrier, flip(opposite(step), m))
+        for m in range(2):
+            signal(barrier, flip(opposite(1), m))
 
     fetch_ops.start()
     fetch_ids.start()
@@ -125,9 +124,19 @@
     def _():
         note()
         pltpu.make_async_copy(data, data, local_sem.at[3]).wait()
-        pl.semaphore_wait(barrier, team + 1)
+        pl.semaphore_wait(barrier, team - 1 + 2 * level)
+
+        @pl.when(level == 1)
+        def _():
+            signal(col_sem, spot)
+
         scatter_near(0)
         pl.semaphore_wait(in_sem, 2)
+
+        @pl.when(level == 0)
+        def _():
+            pl.semaphore_wait(col_sem, 1)
+
         for g in groups[1:]:
             signal(group_sem.at[g // 2 - 1], flip(me, g))
         for c in range(1, chunks):
@@ -165,9 +174,13 @@
         if chunks < 3:
             note()
         pl.semaphore_wait(team_sem, 1)
+        half = len(groups) // 2
         scatter_near(0)
-        scatter_far(chunks - 1, *reversed(groups))
-        for c in range(1, chunks):
+        scatter_far(chunks - 1, *groups[: half - 1 : -1])
+        for c in range(1, min(2, chunks)):
+            scatter_near(c)
+        scatter_far(chunks - 1, *groups[:half][::-1])
+        for c in range(2, chunks):
             scatter_near(c)
 
     fetch_ops.wait()
@@ -280,7 +293,7 @@
         vmem((per, parts * n * shots, traces), data.dtype),
         vmem((n * parts * per + team, shots, traces), data.dtype),
         dma((4,)), dma((2, chunks)), dma, dma, dma((2,)),
-        regular, regular, regular((n // 8 - 1,)),
+        regular, regular, regular, regular((n // 8 - 1,)),
     ]
     anywhere = pl.BlockSpec(memory_space=pl.ANY)
     result = pl.pallas_call(

time: 18 us -> 18 us (level)
  no operation moved by 1% of the time
where the time goes in v4:
time: 18 us; the launch traced here: 17.9 us
  Pallas kernels  17.2 us (96%)
  local copies, waits for them, and re-layouts  0.66 us (4%)
    pallas_call x1, Pallas kernels, per_device(): pl.pallas_call(functools.partial(kernel, n, sizes, finish), out_shape=vme...  17.2 us
    unnamed x1, local copies, waits for them, and re-layouts  0.66 us

profile of v4, /device:TPU:0, one launch (start us, length us, event | category | flops | bytes accessed | tf_op | source)
XLA Modules:
  0.0 17.9 jit_solution(9532911696629091666)
XLA Ops:
  0.0 17.2 %predict.1 = bf16[2,16,4,4,128]{4,3,2,1,0:T(4,128)(2,1)S(1)} custom-call(bf16[2,16,4,4,128]{4,3,2,1,0:T(4,128)(2,1)} %bitcast.3, s32[4,64]{1,0:T(4,128)} %aperture.1, bf16[8,64,64]{2,1,0:T(8,128)(2,1)} %ops.1, s32[2]{0:T(128)} %cable_ops.1), custom_call_target="tpu_custom_call" | custom-call | tf_op jit(solution)/shard_map/predict/pallas_call | solution.py:299
  17.2 0.7 %copy.6 = bf16[2,64,4,128]{3,2,1,0:T(4,128)(2,1)} copy(bf16[2,64,4,128]{3,2,1,0:T(4,128)(2,1)S(1)} %bitcast.2) | data formatting | bytes 262144

commit v5 on v4

--- a/solution.py
+++ b/solution.py
@@ -169,9 +169,9 @@
 
         for c in range(chunks - 1):
             scatter_far(c, *reversed(groups))
-            if c == 1:
+            if c == 0:
                 note()
-        if chunks < 3:
+        if chunks < 2:
             note()
         pl.semaphore_wait(team_sem, 1)
         half = len(groups) // 2

time: 18 us -> 18 us (level)
  no operation moved by 1% of the time
where the time goes in v5:
time: 18 us; the launch traced here: 17.9 us
  Pallas kernels  17.2 us (96%)
  local copies, waits for them, and re-layouts  0.66 us (4%)
    pallas_call x1, Pallas kernels, per_device(): pl.pallas_call(functools.partial(kernel, n, sizes, finish), out_shape=vme...  17.2 us
    unnamed x1, local copies, waits for them, and re-layouts  0.66 us

profile of v5, /device:TPU:0, one launch (start us, length us, event | category | flops | bytes accessed | tf_op | source)
XLA Modules:
  0.0 17.9 jit_solution(17474709543833638243)
XLA Ops:
  0.0 17.2 %predict.1 = bf16[2,16,4,4,128]{4,3,2,1,0:T(4,128)(2,1)S(1)} custom-call(bf16[2,16,4,4,128]{4,3,2,1,0:T(4,128)(2,1)} %bitcast.3, s32[4,64]{1,0:T(4,128)} %aperture.1, bf16[8,64,64]{2,1,0:T(8,128)(2,1)} %ops.1, s32[2]{0:T(128)} %cable_ops.1), custom_call_target="tpu_custom_call" | custom-call | tf_op jit(solution)/shard_map/predict/pallas_call | solution.py:299
  17.2 0.7 %copy.6 = bf16[2,64,4,128]{3,2,1,0:T(4,128)(2,1)} copy(bf16[2,64,4,128]{3,2,1,0:T(4,128)(2,1)S(1)} %bitcast.2) | data formatting | bytes 262144
